TPU v7x, 256 devices: a whole 4x4x8 slice. The times are simulated.
256 devices in a mesh: tm: 32 (over y, z), eval: 8 (over x, core).
Axes of the slice: x: 4, y: 4, z: 8, core: 2. Of those that a mesh axis runs over, the one named last changes fastest.
Arguments:
- hidden: bfloat16 [512, 1024, 1536], P('tm', 'eval'), may hold values from -9 to 9
- modulation: float32 [512, 2, 1536], P('tm'), may hold values from -2 to 3
- head_weight: bfloat16 [64, 1536], replicated, may hold values from -1 to 1
- real_score: bfloat16 [64, 21, 16, 4096], P('eval', None, None, 'tm'), may hold values from -152917 to 152917
- fake_score: bfloat16 [64, 21, 16, 4096], P('eval', None, None, 'tm'), may hold values from -152917 to 152917
- window_start: int32 [64], P('eval'), may hold values from 0 to 491, as said below
- timestep: int32 [64], P('eval'), may hold values from 20 to 999
Outputs:
- d_hidden: bfloat16 [512, 1024, 1536], P('tm', 'eval')
- head_grad: float32 [64, 1536], replicated
- mod_grad: float32 [512, 2, 1536], P('tm')
Inputs may be any that keep to these rules, and one draw needn't show every extreme that they name: `window_start`: every window lies inside the rollout; one window starts at frame 0 and one at the last possible frame.
All inputs are finite; a program needn't handle non-finite values.
Results may differ from a plain program's by a relative error of at most 0.0012.
The roundings to bfloat16 on the way count: a program that leaves them out, or rounds other values in their place, can miss the bound.
Values may be sent and summed in bfloat16 or wider, within the bound.
No kernel may reach another device: no remote copies, remote signals or barrier semaphores. Data moves between devices by JAX's collectives and lax.ppermute only.
A program may use at most 128 MiB of HBM per device.

v0:
```python
import jax
import jax.numpy as jnp
from jax import lax
from jax.sharding import PartitionSpec as P

C = 16
PATCH = 4
WIN = 21
TOK = 1024


def layer_norm(values_in):
    values = values_in.astype(jnp.float32)
    center = jnp.mean(values, axis=-1, keepdims=True)
    shifted = values - center
    inv_std = lax.rsqrt(jnp.mean(shifted * shifted, axis=-1, keepdims=True) + 1e-06)
    return (shifted * inv_std, inv_std)


def per_device(hidden, modulation, head_weight, real_score, fake_score, window_start, timestep):
    frames_dev, tok_dev, width = hidden.shape
    shift = modulation[:, 0][:, None, :]
    scale = modulation[:, 1][:, None, :]
    normed, inv_std = layer_norm(hidden)
    adapted = (normed * (1.0 + scale) + shift).astype(jnp.bfloat16)
    head_out = jnp.einsum("ftd,od->fto", adapted, head_weight, preferred_element_type=jnp.float32)
    latent = head_out.astype(jnp.bfloat16).reshape(frames_dev, tok_dev, C, PATCH)
    latent = latent.transpose(0, 2, 1, 3).reshape(frames_dev, C, tok_dev * PATCH)
    frame_whole = lax.all_gather(latent, "eval", axis=2, tiled=True)
    latent_all = lax.all_to_all(frame_whole, "tm", split_axis=2, concat_axis=0, tiled=True)
    pixel_block = latent_all.shape[2]
    frame_index = window_start[:, None] + jnp.arange(WIN, dtype=jnp.int32)[None, :]
    window_latent = latent_all[frame_index].astype(jnp.float32)
    real_values = real_score.astype(jnp.float32)
    fake_values = fake_score.astype(jnp.float32)
    abs_sums = jnp.sum(jnp.abs(window_latent - real_values), axis=(1, 2, 3))
    totals = lax.psum(abs_sums, "tm")
    normalizer = totals / (WIN * C * PATCH * TOK) + 1e-05
    weight = timestep.astype(jnp.float32) / 1000.0 / normalizer
    window_grad = weight[:, None, None, None] * (fake_values - real_values)
    group_grad = (
        jnp.zeros(latent_all.shape, jnp.float32)
        .at[frame_index.reshape(-1)]
        .add(window_grad.reshape(-1, C, pixel_block))
    )
    home = lax.all_to_all(group_grad, "tm", split_axis=0, concat_axis=2, tiled=True)
    owner_grad = lax.psum_scatter(home, "eval", scatter_dimension=2, tiled=True)
    upstream = owner_grad.reshape(frames_dev, C, tok_dev, PATCH).transpose(0, 2, 1, 3)
    upstream = upstream.reshape(frames_dev, tok_dev, C * PATCH).astype(jnp.bfloat16)
    d_adapted = jnp.einsum("fto,od->ftd", upstream, head_weight, preferred_element_type=jnp.float32)
    head_part = jnp.einsum("fto,ftd->od", upstream, adapted, preferred_element_type=jnp.float32)
    mod_part = jnp.stack([jnp.sum(d_adapted, axis=1), jnp.sum(d_adapted * normed, axis=1)], axis=1)
    head_grad = lax.psum(head_part, ("tm", "eval"))
    mod_grad = lax.psum(mod_part, "eval")
    d_normed = d_adapted * (1.0 + scale)
    d_hidden = inv_std * (
        d_normed
        - jnp.mean(d_normed, axis=-1, keepdims=True)
        - normed * jnp.mean(d_normed * normed, axis=-1, keepdims=True)
    )
    return (d_hidden.astype(jnp.bfloat16), head_grad, mod_grad)


def solution(mesh):
    placed = (
        P("tm", "eval", None),
        P("tm", None, None),
        P(),
        P("eval", None, None, "tm"),
        P("eval", None, None, "tm"),
        P("eval"),
        P("eval"),
    )
    return jax.shard_map(
        per_device,
        mesh=mesh,
        in_specs=placed,
        out_specs=(P("tm", "eval", None), P(), P("tm", None, None)),
        check_vma=False,
    )
```

profile of v0, /device:TPU:1, one launch (start us, length us, event | category | flops | bytes accessed | tf_op | source)
XLA Modules:
  0.0 757.5 jit_solution(7772980234880290092)
XLA Ops:
  7.2 3.8 convert_reduce_fusion
  11.1 4.6 fusion.13
  15.9 3.1 fusion.24
  19.0 3.2 copy.49
  22.2 2.3 copy.50
  24.5 32.2 %all-gather.2.cloned.1.call-done = bf16[16,16,4096]{2,1,0:T(8,128)(2,1)} async-done(((bf16[16,16,512]{2,1,0:T(8,128)(2,1)}), bf16[16,16,4096]{2,1,0:T(8,128)(2,1)}) %all-gather.2.cloned.1.call-update) | async-done | bytes 2097168 | tf_op jit(solution)/shard_map/all_gather | solution.py:29
  56.7 15.4 %copy.51 = bf16[16,16,4096]{1,0,2:T(8,128)(2,1)} copy(bf16[16,16,4096]{2,1,0:T(8,128)(2,1)} %all-gather.2.cloned.1.call-done) | data formatting | bytes 4194304 | tf_op jit(solution)/shard_map/all_gather | solution.py:29
  72.0 20.8 %reshape.132 = bf16[32,2,16384]{2,1,0:T(2,128)(2,1)} reshape(bf16[4096,16,16]{2,1,0:T(8,128)(2,1)} %bitcast.43) | data formatting | bytes 4194304
  92.8 9.6 %all-to-all-start = ((bf16[32,2,16384]{2,1,0:T(2,128)(2,1)}), bf16[32,2,16384]{2,1,0:T(2,128)(2,1)S(1)}, u32[]{:S(2)}, u32[]{:S(2)}) async-start(bf16[32,2,16384]{2,1,0:T(2,128)(2,1)} %reshape.132), calls=%async_computation | async-start | bytes 4194304 | tf_op jit(solution)/shard_map/all_to_all | solution.py:30
  102.8 48.5 %all-to-all-done = bf16[32,2,16384]{2,1,0:T(2,128)(2,1)S(1)} async-done(((bf16[32,2,16384]{2,1,0:T(2,128)(2,1)}), bf16[32,2,16384]{2,1,0:T(2,128)(2,1)S(1)}, u32[]{:S(2)}, u32[]{:S(2)}) %all-to-all-start) | async-done | bytes 2097184 | tf_op jit(solution)/shard_map/all_to_all | solution.py:30
  151.3 14.4 %reshape.133 = bf16[4096,16,16]{2,1,0:T(8,128)(2,1)} reshape(bf16[32,2,16384]{2,1,0:T(2,128)(2,1)S(1)} %all-to-all-done) | data formatting | bytes 4194304
  165.7 14.4 %copy.53 = bf16[32,16,16,128]{3,2,1,0:T(8,128)(2,1)S(1)} copy(bf16[32,16,16,128]{2,1,3,0:T(8,128)(2,1)} %bitcast.44) | data formatting | bytes 4194304 | tf_op jit(solution)/shard_map/all_to_all | solution.py:30
  180.1 1.6 gather_fusion
  181.7 1.4 fusion.22
  183.1 60.2 %psum.21 = f32[8]{0:T(128)S(1)} all-reduce(f32[8]{0:T(128)S(1)} %fusion.22), channel_id=1, replica_groups=mesh['tm'=32,'eval'=8] {'tm'}, use_global_device_ids=true, to_apply=%region_3.0 | all-reduce | flops 8 | bytes 64 | tf_op jit(solution)/shard_map/psum | solution.py:37
  243.4 1.3 fusion.23
  244.7 2.3 broadcast_in_dim.2
  247.0 19.7 %scatter_fusion = f32[512,16,128]{2,1,0:T(8,128)} fusion(f32[512,16,128]{2,1,0:T(8,128)} %broadcast_in_dim.2, s32[168]{0:T(256)S(1)} %bitcast.59, f32[168,16,128]{2,1,0:T(8,128)S(1)} %bitcast.51), kind=kCustom, calls=%fused_computation.1 | custom fusion | flops 344064 | bytes 4129440 | tf_op jit(solution)/shard_map/scatter-add | solution.py:44
  266.7 83.4 %all_to_all.36 = f32[512,16,128]{2,1,0:T(8,128)S(1)} all-to-all(f32[512,16,128]{2,1,0:T(8,128)} %scatter_fusion), channel_id=1, replica_groups=mesh['tm'=32,'eval'=8] {'tm'}, dimensions={0} | all-to-all | bytes 8388608 | tf_op jit(solution)/shard_map/all_to_all | solution.py:46
  350.1 2.5 copy.76
  352.7 50.7 %reduce-scatter.2.cloned.1.call-done = f32[16,16,512]{2,1,0:T(8,128)} async-done(((f32[16,16,4096]{2,1,0:T(8,128)}), f32[16,16,512]{2,1,0:T(8,128)}) %reduce-scatter.2.cloned.1.call-update) | async-done | bytes 524304 | tf_op jit(solution)/shard_map/reduce_scatter | solution.py:47
  403.4 1.1 convert_element_type.43
  404.5 2.8 copy.55
  407.3 4.0 copy.56
  411.3 10.1 %fusion.12 = (f32[16,1536]{1,0:T(8,128)S(1)}, f32[16,128]{1,0:T(8,128)S(1)}, f32[16,128]{1,0:T(8,128)S(1)}, f32[16,1536]{1,0:T(8,128)S(1)}, f32[16,128,1536]{2,1,0:T(8,128)}) fusion(bf16[16,128,1536]{2,1,0:T(8,128)(2,1)} %param.7, f32[16,128]{1,0:T(8,128)S(1)} %add_rsqrt_fusion, f32[16,128]{1,0:T(8,128)S(1)} %broadcast_multiply_fusion.2, ...), kind=kOutput, calls=%fused_computation.16 | convolution fusion | flops 434057216 | bytes 19660800 | tf_op jit(solution)/shard_map/fto,od->ftd/dot_general | solution.py:50
  421.4 3.5 fusion.18
  424.9 0.7 pad_maximum_fusion
  426.2 10.5 %fusion.11 = bf16[16,128,1536]{2,1,0:T(8,128)(2,1)} fusion(bf16[16,128,1536]{2,1,0:T(8,128)(2,1)} %param.7, f32[16,128,1536]{2,1,0:T(8,128)} %get-tuple-element.24, f32[16,128]{1,0:T(8,128)S(1)} %broadcast_multiply_fusion, f32[16,128]{1,0:T(8,128)S(1)} %broadcast_multiply_fusion.1, f32[16,1536]{1,0:T(8,128)S(1)} %get-tuple-element.26, ...), kind=kLoop, calls=%fused_computation.15 | loop fusion | flops 28311552 | bytes 25296896 | tf_op jit(solution)/shard_map/convert_element_type | solution.py:61
  436.7 53.9 %all-reduce.5.cloned.1.call-done = f32[16,2,1536]{2,0,1:T(8,128)} async-done(((f32[16,2,1536]{2,0,1:T(8,128)}), f32[16,2,1536]{2,0,1:T(8,128)}) %all-reduce.5.cloned.1.call-update) | async-done | bytes 196624 | tf_op jit(solution)/shard_map/psum | solution.py:54
  490.5 1.8 copy.59
  492.3 256.9 %all-reduce.3.cloned.1.call-done = f32[64,1536]{1,0:T(8,128)} async-done(((f32[64,1536]{1,0:T(8,128)}), f32[64,1536]{1,0:T(8,128)}) %all-reduce.3.cloned.1.call-update) | async-done | bytes 393232 | tf_op jit(solution)/shard_map/psum | solution.py:53
  749.2 1.8 copy.80
  (38 shorter events, 1.3 us)
Async XLA Ops:
  7.2 8.7 %copy-start = (bf16[64,1536]{1,0:T(8,128)(2,1)S(1)}, bf16[64,1536]{1,0:T(8,128)(2,1)}, u32[]{:S(2)}) copy-start(bf16[64,1536]{1,0:T(8,128)(2,1)} %param.9) | copy-start | bytes 589828
  7.2 8.5 %copy-start.3 = (f32[16,2,1536]{2,1,0:T(2,128)S(1)}, f32[16,2,1536]{2,1,0:T(2,128)}, u32[]{:S(2)}) copy-start(f32[16,2,1536]{2,1,0:T(2,128)} %param.8) | copy-start | bytes 589828
  7.2 49.5 %all-gather.2.cloned.1.call-start = ((), (), s32[]{:S(2)}) async-start(), calls=%async_computation.3 | async-start | bytes 2359296 | tf_op jit(solution)/shard_map/all_gather | solution.py:29
  7.2 8.7 %copy-start.1 = (bf16[16,128,1536]{2,1,0:T(8,128)(2,1)S(1)}, bf16[16,128,1536]{2,1,0:T(8,128)(2,1)}, u32[]{:S(2)}) copy-start(bf16[16,128,1536]{2,1,0:T(8,128)(2,1)} %param.7) | copy-start | bytes 18874372
  72.0 30.4 %copy-start.4 = (s32[8]{0:T(128)S(1)}, s32[8]{0:T(128)}, u32[]{:S(2)}) copy-start(s32[8]{0:T(128)} %param.12) | copy-start | bytes 100
  92.8 58.5 %all-to-all-start = ((bf16[32,2,16384]{2,1,0:T(2,128)(2,1)}), bf16[32,2,16384]{2,1,0:T(2,128)(2,1)S(1)}, u32[]{:S(2)}, u32[]{:S(2)}) async-start(bf16[32,2,16384]{2,1,0:T(2,128)(2,1)} %reshape.132), calls=%async_computation | async-start | bytes 4194304 | tf_op jit(solution)/shard_map/all_to_all | solution.py:30
  102.4 301.0 %reduce-scatter.2.cloned.1.call-start = ((), (), s32[]{:S(2)}) async-start(), calls=%async_computation.4 | async-start | bytes 4718592 | tf_op jit(solution)/shard_map/reduce_scatter | solution.py:47
  165.7 16.0 %copy-start.2 = (bf16[8,21,16,128]{3,2,1,0:T(8,128)(2,1)S(1)}, bf16[8,21,16,128]{3,2,1,0:T(8,128)(2,1)}, u32[]{:S(2)}) copy-start(bf16[8,21,16,128]{3,2,1,0:T(8,128)(2,1)} %param.10) | copy-start | bytes 2064388
  165.7 77.7 %copy-start.5 = (s32[8]{0:T(128)S(1)}, s32[8]{0:T(128)}, u32[]{:S(2)}) copy-start(s32[8]{0:T(128)} %param.13) | copy-start | bytes 100
  352.7 137.9 %all-reduce.5.cloned.1.call-start = ((), (), s32[]{:S(2)}) async-start(), calls=%async_computation.6 | async-start | bytes 393216 | tf_op jit(solution)/shard_map/psum | solution.py:54
  407.3 14.2 %slice-start = ((s8[6291456]{0:T(1024)(128)(4,1)}), s8[2097152]{0:T(1024)(128)(4,1)S(1)}, s32[]{:S(2)}) async-start(s8[6291456]{0:T(1024)(128)(4,1)} %bitcast.45), calls=%async_computation.7 | async-start | bytes 4194304
  411.3 10.1 %slice-start.1 = ((s8[6291456]{0:T(1024)(128)(4,1)}), s8[4194304]{0:T(1024)(128)(4,1)S(1)}, s32[]{:S(2)}) async-start(s8[6291456]{0:T(1024)(128)(4,1)} %bitcast.45), calls=%async_computation.8 | async-start | bytes 8388608
  425.6 323.6 %all-reduce.3.cloned.1.call-start = ((), (), s32[]{:S(2)}) async-start(), calls=%async_computation.5 | async-start | bytes 786432 | tf_op jit(solution)/shard_map/psum | solution.py:53
Sparse Core Ops, SparseCore 0:
  24.6 31.9 all-gather.1
  352.8 50.5 reduce-scatter.1
  425.7 64.7 all-reduce.4
  496.5 252.6 all-reduce.2
where the time goes:
time: 760 us; the launch traced here: 758 us
  waiting for transfers between devices  443 us (58%)
  blocking collectives  144 us (19%)
  local copies, waits for them, and re-layouts  87.5 us (12%)
  other arithmetic  43.3 us (6%)
  matrix products  16.6 us (2%)
  between operations  14 us (2%)
  starting transfers between devices  9.73 us (1%)
    psum x1, waiting for transfers between devices, per_device(): head_grad = lax.psum(head_part, ('tm', 'eval'))  257 us
    all_to_all x1, blocking collectives, per_device(): lax.all_to_all(group_grad, 'tm', split_axis=0, concat_axis=2, tiled=True)  83.4 us
    psum x1, blocking collectives, per_device(): totals = lax.psum(abs_sums, 'tm')  60.2 us
    psum x1, waiting for transfers between devices, per_device(): mod_grad = lax.psum(mod_part, 'eval')  53.9 us
    reduce_scatter x1, waiting for transfers between devices, per_device(): owner_grad = lax.psum_scatter(home, 'eval', scatter_dimension=2, tiled=True)  50.7 us
    all_to_all x1, waiting for transfers between devices, per_device(): lax.all_to_all(frame_whole, 'tm', split_axis=2, concat_axis=0, tiled=True)  48.5 us
    unnamed x20, local copies, waits for them, and re-layouts  38.7 us
    all_gather x1, waiting for transfers between devices, per_device(): frame_whole = lax.all_gather(latent, 'eval', axis=2, tiled=True)  32.2 us
  transfers between devices with their start and end apart: 5, of which 5 were waited for; matrix products, arithmetic and copies ran while one was open for 2% of the time, Pallas kernels for 0%

commit v1 on v0

--- a/solution.py
+++ b/solution.py
@@ -7,6 +7,11 @@
 PATCH = 4
 WIN = 21
 TOK = 1024
+
+
+def axis_by_axis(value, first, second):
+    inner = lax.psum(value, first)
+    return lax.psum(inner, second)
 
 
 def layer_norm(values_in):
@@ -50,7 +55,7 @@
     d_adapted = jnp.einsum("fto,od->ftd", upstream, head_weight, preferred_element_type=jnp.float32)
     head_part = jnp.einsum("fto,ftd->od", upstream, adapted, preferred_element_type=jnp.float32)
     mod_part = jnp.stack([jnp.sum(d_adapted, axis=1), jnp.sum(d_adapted * normed, axis=1)], axis=1)
-    head_grad = lax.psum(head_part, ("tm", "eval"))
+    head_grad = axis_by_axis(head_part, "tm", "eval")
     mod_grad = lax.psum(mod_part, "eval")
     d_normed = d_adapted * (1.0 + scale)
     d_hidden = inv_std * (

time: 760 us -> 652 us (0.86)
  waiting for transfers between devices: 443 us -> 334 us
    psum x2, waiting for transfers between devices: 311 us -> 202 us  [the longest x1 143 us: axis_by_axis(): inner = lax.psum(value, first)]
where the time goes in v1:
time: 652 us; the launch traced here: 648 us
  waiting for transfers between devices  334 us (51%)
  blocking collectives  144 us (22%)
  local copies, waits for them, and re-layouts  87.5 us (13%)
  other arithmetic  43.3 us (7%)
  matrix products  16.6 us (3%)
  between operations  14 us (2%)
  starting transfers between devices  9.73 us (1%)
    psum x1, waiting for transfers between devices, axis_by_axis(): inner = lax.psum(value, first)  143 us
    all_to_all x1, blocking collectives, per_device(): lax.all_to_all(group_grad, 'tm', split_axis=0, concat_axis=2, tiled=True)  83.4 us
    psum x1, blocking collectives, per_device(): totals = lax.psum(abs_sums, 'tm')  60.2 us
    psum x1, waiting for transfers between devices, axis_by_axis(): return lax.psum(inner, second)  58.7 us
    reduce_scatter x1, waiting for transfers between devices, per_device(): owner_grad = lax.psum_scatter(home, 'eval', scatter_dimension=2, tiled=True)  50.7 us
    all_to_all x1, waiting for transfers between devices, per_device(): lax.all_to_all(frame_whole, 'tm', split_axis=2, concat_axis=0, tiled=True)  48.5 us
    unnamed x20, local copies, waits for them, and re-layouts  38.7 us
    all_gather x1, waiting for transfers between devices, per_device(): frame_whole = lax.all_gather(latent, 'eval', axis=2, tiled=True)  32.2 us
  transfers between devices with their start and end apart: 5, of which 5 were waited for; matrix products, arithmetic and copies ran while one was open for 2% of the time, Pallas kernels for 0%

profile of v1, /device:TPU:1, one launch (start us, length us, event | category | flops | bytes accessed | tf_op | source)
XLA Modules:
  0.0 648.4 jit_solution(8560909026480814417)
XLA Ops:
  7.2 3.8 convert_reduce_fusion
  11.1 4.6 fusion.13
  15.9 3.1 fusion.24
  19.0 3.2 copy.49
  22.2 2.3 copy.50
  24.5 32.2 %all-gather.2.cloned.1.call-done = bf16[16,16,4096]{2,1,0:T(8,128)(2,1)} async-done(((bf16[16,16,512]{2,1,0:T(8,128)(2,1)}), bf16[16,16,4096]{2,1,0:T(8,128)(2,1)}) %all-gather.2.cloned.1.call-update) | async-done | bytes 2097168 | tf_op jit(solution)/shard_map/all_gather | solution.py:34
  56.7 15.4 %copy.51 = bf16[16,16,4096]{1,0,2:T(8,128)(2,1)} copy(bf16[16,16,4096]{2,1,0:T(8,128)(2,1)} %all-gather.2.cloned.1.call-done) | data formatting | bytes 4194304 | tf_op jit(solution)/shard_map/all_gather | solution.py:34
  72.0 20.8 %reshape.132 = bf16[32,2,16384]{2,1,0:T(2,128)(2,1)} reshape(bf16[4096,16,16]{2,1,0:T(8,128)(2,1)} %bitcast.43) | data formatting | bytes 4194304
  92.8 9.6 %all-to-all-start = ((bf16[32,2,16384]{2,1,0:T(2,128)(2,1)}), bf16[32,2,16384]{2,1,0:T(2,128)(2,1)S(1)}, u32[]{:S(2)}, u32[]{:S(2)}) async-start(bf16[32,2,16384]{2,1,0:T(2,128)(2,1)} %reshape.132), calls=%async_computation | async-start | bytes 4194304 | tf_op jit(solution)/shard_map/all_to_all | solution.py:35
  102.8 48.5 %all-to-all-done = bf16[32,2,16384]{2,1,0:T(2,128)(2,1)S(1)} async-done(((bf16[32,2,16384]{2,1,0:T(2,128)(2,1)}), bf16[32,2,16384]{2,1,0:T(2,128)(2,1)S(1)}, u32[]{:S(2)}, u32[]{:S(2)}) %all-to-all-start) | async-done | bytes 2097184 | tf_op jit(solution)/shard_map/all_to_all | solution.py:35
  151.3 14.4 %reshape.133 = bf16[4096,16,16]{2,1,0:T(8,128)(2,1)} reshape(bf16[32,2,16384]{2,1,0:T(2,128)(2,1)S(1)} %all-to-all-done) | data formatting | bytes 4194304
  165.7 14.4 %copy.53 = bf16[32,16,16,128]{3,2,1,0:T(8,128)(2,1)S(1)} copy(bf16[32,16,16,128]{2,1,3,0:T(8,128)(2,1)} %bitcast.44) | data formatting | bytes 4194304 | tf_op jit(solution)/shard_map/all_to_all | solution.py:35
  180.1 1.6 gather_fusion
  181.7 1.4 fusion.22
  183.1 60.2 %psum.28 = f32[8]{0:T(128)S(1)} all-reduce(f32[8]{0:T(128)S(1)} %fusion.22), channel_id=1, replica_groups=mesh['tm'=32,'eval'=8] {'tm'}, use_global_device_ids=true, to_apply=%region_3.0 | all-reduce | flops 8 | bytes 64 | tf_op jit(solution)/shard_map/psum | solution.py:42
  243.4 1.3 fusion.23
  244.7 2.3 broadcast_in_dim.2
  247.0 19.7 %scatter_fusion = f32[512,16,128]{2,1,0:T(8,128)} fusion(f32[512,16,128]{2,1,0:T(8,128)} %broadcast_in_dim.2, s32[168]{0:T(256)S(1)} %bitcast.59, f32[168,16,128]{2,1,0:T(8,128)S(1)} %bitcast.51), kind=kCustom, calls=%fused_computation.1 | custom fusion | flops 344064 | bytes 4129440 | tf_op jit(solution)/shard_map/scatter-add | solution.py:49
  266.7 83.4 %all_to_all.36 = f32[512,16,128]{2,1,0:T(8,128)S(1)} all-to-all(f32[512,16,128]{2,1,0:T(8,128)} %scatter_fusion), channel_id=1, replica_groups=mesh['tm'=32,'eval'=8] {'tm'}, dimensions={0} | all-to-all | bytes 8388608 | tf_op jit(solution)/shard_map/all_to_all | solution.py:51
  350.1 2.5 copy.76
  352.7 50.7 %reduce-scatter.2.cloned.1.call-done = f32[16,16,512]{2,1,0:T(8,128)} async-done(((f32[16,16,4096]{2,1,0:T(8,128)}), f32[16,16,512]{2,1,0:T(8,128)}) %reduce-scatter.2.cloned.1.call-update) | async-done | bytes 524304 | tf_op jit(solution)/shard_map/reduce_scatter | solution.py:52
  403.4 1.1 convert_element_type.43
  404.5 2.8 copy.55
  407.3 4.0 copy.56
  411.3 10.1 %fusion.12 = (f32[16,1536]{1,0:T(8,128)S(1)}, f32[16,128]{1,0:T(8,128)S(1)}, f32[16,128]{1,0:T(8,128)S(1)}, f32[16,1536]{1,0:T(8,128)S(1)}, f32[16,128,1536]{2,1,0:T(8,128)}) fusion(bf16[16,128,1536]{2,1,0:T(8,128)(2,1)} %param.7, f32[16,128]{1,0:T(8,128)S(1)} %add_rsqrt_fusion, f32[16,128]{1,0:T(8,128)S(1)} %broadcast_multiply_fusion.2, ...), kind=kOutput, calls=%fused_computation.16 | convolution fusion | flops 434057216 | bytes 19660800 | tf_op jit(solution)/shard_map/fto,od->ftd/dot_general | solution.py:55
  421.4 3.5 fusion.18
  425.0 0.7 pad_maximum_fusion
  425.7 143.4 %all-reduce.4.cloned.1.call-done = f32[64,1536]{1,0:T(8,128)} async-done(((f32[64,1536]{1,0:T(8,128)}), f32[64,1536]{1,0:T(8,128)}) %all-reduce.4.cloned.1.call-update) | async-done | bytes 393232 | tf_op jit(solution)/shard_map/psum | solution.py:13
  569.1 10.5 %fusion.11 = bf16[16,128,1536]{2,1,0:T(8,128)(2,1)} fusion(bf16[16,128,1536]{2,1,0:T(8,128)(2,1)} %param.7, f32[16,128,1536]{2,1,0:T(8,128)} %get-tuple-element.26, f32[16,128]{1,0:T(8,128)S(1)} %broadcast_multiply_fusion, f32[16,128]{1,0:T(8,128)S(1)} %broadcast_multiply_fusion.1, f32[16,1536]{1,0:T(8,128)S(1)} %get-tuple-element.28, ...), kind=kLoop, calls=%fused_computation.15 | loop fusion | flops 28311552 | bytes 25296896 | tf_op jit(solution)/shard_map/convert_element_type | solution.py:66
  579.6 58.7 %all-reduce.6.cloned.1.call-done = (f32[64,1536]{1,0:T(8,128)}, f32[16,2,1536]{2,0,1:T(8,128)}) async-done(((f32[64,1536]{1,0:T(8,128)}, f32[16,2,1536]{2,0,1:T(8,128)}), (f32[64,1536]{1,0:T(8,128)}, f32[16,2,1536]{2,0,1:T(8,128)})) %all-reduce.6.cloned.1.call-update) | async-done | bytes 589840 | tf_op jit(solution)/shard_map/psum | solution.py:14
  638.3 1.8 copy.59
  640.0 1.8 copy.81
  (38 shorter events, 0.8 us)
Async XLA Ops:
  7.2 8.7 %copy-start = (bf16[64,1536]{1,0:T(8,128)(2,1)S(1)}, bf16[64,1536]{1,0:T(8,128)(2,1)}, u32[]{:S(2)}) copy-start(bf16[64,1536]{1,0:T(8,128)(2,1)} %param.9) | copy-start | bytes 589828
  7.2 8.5 %copy-start.3 = (f32[16,2,1536]{2,1,0:T(2,128)S(1)}, f32[16,2,1536]{2,1,0:T(2,128)}, u32[]{:S(2)}) copy-start(f32[16,2,1536]{2,1,0:T(2,128)} %param.8) | copy-start | bytes 589828
  7.2 49.5 %all-gather.2.cloned.1.call-start = ((), (), s32[]{:S(2)}) async-start(), calls=%async_computation.3 | async-start | bytes 2359296 | tf_op jit(solution)/shard_map/all_gather | solution.py:34
  7.2 8.7 %copy-start.1 = (bf16[16,128,1536]{2,1,0:T(8,128)(2,1)S(1)}, bf16[16,128,1536]{2,1,0:T(8,128)(2,1)}, u32[]{:S(2)}) copy-start(bf16[16,128,1536]{2,1,0:T(8,128)(2,1)} %param.7) | copy-start | bytes 18874372
  72.0 30.4 %copy-start.4 = (s32[8]{0:T(128)S(1)}, s32[8]{0:T(128)}, u32[]{:S(2)}) copy-start(s32[8]{0:T(128)} %param.12) | copy-start | bytes 100
  92.8 58.5 %all-to-all-start = ((bf16[32,2,16384]{2,1,0:T(2,128)(2,1)}), bf16[32,2,16384]{2,1,0:T(2,128)(2,1)S(1)}, u32[]{:S(2)}, u32[]{:S(2)}) async-start(bf16[32,2,16384]{2,1,0:T(2,128)(2,1)} %reshape.132), calls=%async_computation | async-start | bytes 4194304 | tf_op jit(solution)/shard_map/all_to_all | solution.py:35
  102.4 301.0 %reduce-scatter.2.cloned.1.call-start = ((), (), s32[]{:S(2)}) async-start(), calls=%async_computation.4 | async-start | bytes 4718592 | tf_op jit(solution)/shard_map/reduce_scatter | solution.py:52
  165.7 16.0 %copy-start.2 = (bf16[8,21,16,128]{3,2,1,0:T(8,128)(2,1)S(1)}, bf16[8,21,16,128]{3,2,1,0:T(8,128)(2,1)}, u32[]{:S(2)}) copy-start(bf16[8,21,16,128]{3,2,1,0:T(8,128)(2,1)} %param.10) | copy-start | bytes 2064388
  165.7 77.7 %copy-start.5 = (s32[8]{0:T(128)S(1)}, s32[8]{0:T(128)}, u32[]{:S(2)}) copy-start(s32[8]{0:T(128)} %param.13) | copy-start | bytes 100
  352.7 216.4 %all-reduce.4.cloned.1.call-start = ((), (), s32[]{:S(2)}) async-start(), calls=%async_computation.5 | async-start | bytes 786432 | tf_op jit(solution)/shard_map/psum | solution.py:13
  407.3 14.2 %slice-start = ((s8[6291456]{0:T(1024)(128)(4,1)}), s8[2097152]{0:T(1024)(128)(4,1)S(1)}, s32[]{:S(2)}) async-start(s8[6291456]{0:T(1024)(128)(4,1)} %bitcast.45), calls=%async_computation.7 | async-start | bytes 4194304
  411.3 10.1 %slice-start.1 = ((s8[6291456]{0:T(1024)(128)(4,1)}), s8[4194304]{0:T(1024)(128)(4,1)S(1)}, s32[]{:S(2)}) async-start(s8[6291456]{0:T(1024)(128)(4,1)} %bitcast.45), calls=%async_computation.8 | async-start | bytes 8388608
  424.9 213.4 %all-reduce.6.cloned.1.call-start = ((), (), s32[]{:S(2)}) async-start(), calls=%async_computation.6 | async-start | bytes 1179648 | tf_op jit(solution)/shard_map/psum | solution.py:14
Sparse Core Ops, SparseCore 0:
  24.6 31.9 all-gather.1
  352.8 50.5 reduce-scatter.1
  425.0 144.0 all-reduce.3
  572.0 66.2 all-reduce.5
